TPU v7x, 32 devices: a whole 2x2x4 slice. The times are simulated.
32 devices in a mesh: row: 8 (over y, x, core), col: 4 (over z).
Axes of the slice: x: 2, y: 2, z: 4, core: 2. Of those that a mesh axis runs over, the one named last changes fastest.
Arguments:
- activations: bfloat16 [1024, 8192], P(None, 'row'), may hold values from -10 to 10
- cotangents: bfloat16 [1024, 8192], P(None, 'row'), may hold values from -10 to 10
- act_factor: bfloat16 [8192, 8192], P('row', 'col'), may hold values from -0.5 to 1.5
- grad_factor: bfloat16 [8192, 8192], P('row', 'col'), may hold values from -0.5 to 1.5
Outputs:
- act_updated: bfloat16 [8192, 8192], P('row', 'col')
- grad_updated: bfloat16 [8192, 8192], P('row', 'col')
All inputs are finite; a program needn't handle non-finite values.
Results may differ from a plain program's by a relative error of at most 0.0057.
Values may be sent and summed in bfloat16 or wider, within the bound.
A program may use at most 128 MiB of HBM per device.

v0:
```python
import jax
import jax.numpy as jnp
from jax import lax
from jax.sharding import PartitionSpec as P

D = 8192
TOKENS = 1024


keep_scale = 1.45
gram_scale = 0.5


def times_transposed(factor_block, projected):
    return lax.dot_general(
        factor_block, projected, (((1,), (1,)), ((), ())), preferred_element_type=jnp.float32
    )


def local(activations, cotangents, act_factor, grad_factor):
    width = act_factor.shape[1]
    token_count = activations.shape[0]
    own_rows = lax.psum_scatter(
        jnp.concatenate(
            [
                jnp.dot(activations, act_factor, preferred_element_type=jnp.float32),
                jnp.dot(cotangents, grad_factor, preferred_element_type=jnp.float32),
            ],
            axis=1,
        ),
        "row",
        scatter_dimension=0,
        tiled=True,
    ).astype(jnp.bfloat16)
    projected = lax.all_gather(own_rows, "row", axis=0, tiled=True)
    squares = jnp.square(own_rows.astype(jnp.float32))
    act_total, grad_total = lax.psum(
        (jnp.sum(squares[:, :width]), jnp.sum(squares[:, width:])), ("row", "col")
    )
    act_mean = act_total / (TOKENS * D)
    grad_mean = grad_total / (TOKENS * D)
    act_proj = projected[:, :width]
    grad_proj = projected[:, width:]
    own_images = lax.psum_scatter(
        jnp.concatenate(
            [times_transposed(act_factor, act_proj), times_transposed(grad_factor, grad_proj)],
            axis=1,
        ),
        "col",
        scatter_dimension=0,
        tiled=True,
    ).astype(jnp.bfloat16)
    both_images = lax.all_gather(own_images, "col", axis=0, tiled=True)
    act_image = both_images[:, :token_count]
    grad_image = both_images[:, token_count:]
    act_change = jnp.dot(act_image, act_proj, preferred_element_type=jnp.float32)
    grad_change = jnp.dot(grad_image, grad_proj, preferred_element_type=jnp.float32)
    act_updated = (
        keep_scale * act_factor.astype(jnp.float32) - gram_scale * grad_mean / TOKENS * act_change
    ).astype(jnp.bfloat16)
    grad_updated = (
        keep_scale * grad_factor.astype(jnp.float32) - gram_scale * act_mean / TOKENS * grad_change
    ).astype(jnp.bfloat16)
    return (act_updated, grad_updated)


def solution(mesh):
    return jax.shard_map(
        local,
        mesh=mesh,
        in_specs=(P(None, "row"), P(None, "row"), P("row", "col"), P("row", "col")),
        out_specs=(P("row", "col"), P("row", "col")),
        check_vma=False,
    )
```

profile of v0, /device:TPU:0, one launch (start us, length us, event | category | flops | bytes accessed | tf_op | source)
XLA Modules:
  0.0 475.5 jit_solution(11034483147673324875)
XLA Ops:
  7.2 0.0 copy-start
  7.2 0.0 reduce-scatter.3.cloned.1.call-start
  7.2 1.5 copy-done
  8.8 0.0 copy-start.3
  8.8 0.0 copy-start.7
  8.8 6.4 %fusion.14 = f32[1024,2048]{1,0:T(8,128)S(1)} fusion(bf16[1024,1024]{1,0:T(8,128)(2,1)S(1)} %copy-done, bf16[1024,2048]{1,0:T(8,128)(2,1)} %param.6), kind=kOutput, calls=%fused_computation.17 | convolution fusion | flops 4294967296 | bytes 14680064 | tf_op jit(solution)/shard_map/dot_general | solution.py:26
  15.2 0.0 copy-done.3
  15.2 0.0 copy-done.7
  15.2 4.5 fusion.15
  19.7 6.2 %pad_maximum_fusion = f32[1024,4096]{1,0:T(8,128)} fusion(f32[1024,2048]{1,0:T(8,128)S(1)} %fusion.15, f32[1024,2048]{1,0:T(8,128)S(1)} %fusion.14), kind=kLoop, calls=%fused_computation | loop fusion | flops 4194304 | bytes 33554432 | tf_op jit(solution)/shard_map/concatenate | solution.py:24
  26.0 0.0 reduce-scatter.3.cloned.1.call-update
  26.0 0.0 all-gather.3.cloned.1.call-start
  26.0 119.0 %reduce-scatter.3.cloned.1.call-done = f32[128,4096]{1,0:T(8,128)} async-done(((f32[1024,4096]{1,0:T(8,128)}), f32[128,4096]{1,0:T(8,128)}) %reduce-scatter.3.cloned.1.call-update) | async-done | bytes 2097168 | tf_op jit(solution)/shard_map/reduce_scatter | solution.py:23
  145.1 2.9 convert_multiply_fusion
  147.9 0.0 all-gather.3.cloned.1.call-update
  148.0 0.2 reduce-scatter.5.cloned.1.call-start
  148.2 54.2 %all-gather.3.cloned.1.call-done = bf16[1024,4096]{1,0:T(8,128)(2,1)} async-done(((bf16[128,4096]{1,0:T(8,128)(2,1)}), bf16[1024,4096]{1,0:T(8,128)(2,1)}) %all-gather.3.cloned.1.call-update) | async-done | bytes 8388624 | tf_op jit(solution)/shard_map/all_gather | solution.py:35
  202.4 0.0 copy-start.2
  202.4 0.0 copy-start.4
  202.4 7.7 %fusion.9 = f32[1024,1024]{0,1:T(8,128)S(1)} fusion(bf16[1024,2048]{1,0:T(8,128)(2,1)} %param.7, bf16[1024,4096]{1,0:T(8,128)(2,1)} %all-gather.3.cloned.1.call-done), kind=kOutput, calls=%fused_computation.11 | convolution fusion | flops 4294967296 | bytes 12582912 | tf_op jit(solution)/shard_map/dot_general | solution.py:15
  210.1 0.0 copy-done.2
  210.1 0.0 copy-done.4
  210.1 4.5 fusion.6
  214.7 4.1 pad_maximum_fusion.1
  218.8 0.0 reduce-scatter.5.cloned.1.call-update
  218.8 0.0 all-gather.5.cloned.1.call-start
  218.8 144.7 %reduce-scatter.5.cloned.1.call-done = f32[256,2048]{0,1:T(8,128)} async-done(((f32[1024,2048]{0,1:T(8,128)}), f32[256,2048]{0,1:T(8,128)}) %reduce-scatter.5.cloned.1.call-update) | async-done | bytes 2097168 | tf_op jit(solution)/shard_map/reduce_scatter | solution.py:44
  363.5 2.7 convert_element_type.24
  366.2 0.0 all-gather.5.cloned.1.call-update
  366.2 0.9 slice_reduce_fusion
  367.1 59.0 %all-reduce = (f32[]{:T(128)}, f32[]{:T(128)}) all-reduce(f32[]{:T(128)} %get-tuple-element.3, f32[]{:T(128)} %get-tuple-element.2), channel_id=1, replica_groups=mesh['row'=8,'col'=4] {'row','col'}, use_global_device_ids=true, to_apply=%region_2.0 | all-reduce | flops 2 | bytes 16 | tf_op jit(solution)/shard_map/psum | solution.py:37
  427.4 21.2 %all-gather.5.cloned.1.call-done = bf16[1024,2048]{0,1:T(8,128)(2,1)} async-done(((bf16[256,2048]{0,1:T(8,128)(2,1)}), bf16[1024,2048]{0,1:T(8,128)(2,1)}) %all-gather.5.cloned.1.call-update) | async-done | bytes 4194320 | tf_op jit(solution)/shard_map/all_gather | solution.py:53
  448.6 0.0 copy-start.5
  448.6 0.0 copy-start.6
  448.6 11.3 %subtract_convert_fusion = bf16[1024,2048]{1,0:T(8,128)(2,1)} fusion(bf16[1024,2048]{1,0:T(8,128)(2,1)} %param.7, f32[]{:T(128)S(6)} %div.9, bf16[1024,4096]{1,0:T(8,128)(2,1)} %all-gather.3.cloned.1.call-done, bf16[1024,2048]{0,1:T(8,128)(2,1)} %all-gather.5.cloned.1.call-done), kind=kOutput, calls=%fused_computation.2 | convolution fusion | flops 4305453056 | bytes 14680068 | tf_op jit(solution)/shard_map/dot_general | solution.py:57
  459.9 0.0 copy-done.5
  459.9 0.0 copy-done.6
  459.9 0.0 copy-start.1
  459.9 9.1 %subtract_convert_fusion.1 = bf16[1024,2048]{1,0:T(8,128)(2,1)} fusion(bf16[1024,2048]{1,0:T(8,128)(2,1)S(1)} %copy-done.5, f32[]{:T(128)S(6)} %div.8, bf16[1024,4096]{1,0:T(8,128)(2,1)} %all-gather.3.cloned.1.call-done, bf16[1024,2048]{0,1:T(8,128)(2,1)S(1)} %copy-done.6), kind=kOutput, calls=%fused_computation.3 | convolution fusion | flops 4305453056 | bytes 14680068 | tf_op jit(solution)/shard_map/dot_general | solution.py:56
  469.0 0.0 copy-done.1
Async XLA Ops:
  7.2 1.6 copy-start
  7.2 137.9 %reduce-scatter.3.cloned.1.call-start = ((), (), s32[]{:S(2)}) async-start(), calls=%async_computation.2 | async-start | bytes 18874368 | tf_op jit(solution)/shard_map/reduce_scatter | solution.py:23
  8.8 6.4 %copy-start.3 = (bf16[1024,2048]{1,0:T(8,128)(2,1)S(1)}, bf16[1024,2048]{1,0:T(8,128)(2,1)}, u32[]{:S(2)}) copy-start(bf16[1024,2048]{1,0:T(8,128)(2,1)} %param.7) | copy-start | bytes 12582916
  8.8 6.4 %copy-start.7 = (bf16[1024,1024]{1,0:T(8,128)(2,1)S(1)}, bf16[1024,1024]{1,0:T(8,128)(2,1)}, u32[]{:S(2)}) copy-start(bf16[1024,1024]{1,0:T(8,128)(2,1)} %param.5) | copy-start | bytes 6291460
  26.0 176.4 %all-gather.3.cloned.1.call-start = ((), (), s32[]{:S(2)}) async-start(), calls=%async_computation.3 | async-start | bytes 9437184 | tf_op jit(solution)/shard_map/all_gather | solution.py:35
  148.0 215.6 %reduce-scatter.5.cloned.1.call-start = ((), (), s32[]{:S(2)}) async-start(), calls=%async_computation.4 | async-start | bytes 10485760 | tf_op jit(solution)/shard_map/reduce_scatter | solution.py:44
  202.4 7.7 %copy-start.2 = (bf16[1024,4096]{1,0:T(8,128)(2,1)S(1)}, bf16[1024,4096]{1,0:T(8,128)(2,1)}, u32[]{:S(2)}) copy-start(bf16[1024,4096]{1,0:T(8,128)(2,1)} %all-gather.3.cloned.1.call-done) | copy-start | bytes 25165828
  202.4 7.8 %copy-start.4 = (bf16[1024,2048]{1,0:T(8,128)(2,1)S(1)}, bf16[1024,2048]{1,0:T(8,128)(2,1)}, u32[]{:S(2)}) copy-start(bf16[1024,2048]{1,0:T(8,128)(2,1)} %param.6) | copy-start | bytes 12582916
  218.8 229.8 %all-gather.5.cloned.1.call-start = ((), (), s32[]{:S(2)}) async-start(), calls=%async_computation.5 | async-start | bytes 5242880 | tf_op jit(solution)/shard_map/all_gather | solution.py:53
  448.6 11.3 %copy-start.5 = (bf16[1024,2048]{1,0:T(8,128)(2,1)S(1)}, bf16[1024,2048]{1,0:T(8,128)(2,1)}, u32[]{:S(2)}) copy-start(bf16[1024,2048]{1,0:T(8,128)(2,1)} %param.6) | copy-start | bytes 12582916
  448.6 11.3 %copy-start.6 = (bf16[1024,2048]{0,1:T(8,128)(2,1)S(1)}, bf16[1024,2048]{0,1:T(8,128)(2,1)}, u32[]{:S(2)}) copy-start(bf16[1024,2048]{0,1:T(8,128)(2,1)} %all-gather.5.cloned.1.call-done) | copy-start | bytes 12582916
  459.9 9.1 %copy-start.1 = (bf16[1024,1024]{1,0:T(8,128)(2,1)S(1)}, bf16[1024,1024]{1,0:T(8,128)(2,1)}, u32[]{:S(2)}) copy-start(bf16[1024,1024]{1,0:T(8,128)(2,1)} %param.4) | copy-start | bytes 6291460
Sparse Core Ops, SparseCore 0:
  26.1 118.9 reduce-scatter.2
  148.1 54.2 all-gather.2
  218.9 144.6 reduce-scatter.4
  366.4 82.1 all-gather.4
where the time goes:
time: 476 us
  waiting for transfers between devices  339 us (71%)
  blocking collectives  59 us (12%)
  matrix products  43.6 us (9%)
  other arithmetic  16.7 us (4%)
  between operations  15.1 us (3%)
    reduce_scatter x1, waiting for transfers between devices, local(): lax.psum_scatter(jnp.concatenate([times_transposed(act_factor, act_proj),...  145 us
    reduce_scatter x1, waiting for transfers between devices, local(): lax.psum_scatter(jnp.concatenate([jnp.dot(activations, act_factor, prefer...  119 us
    psum x1, blocking collectives, local(): lax.psum((jnp.sum(squares[:, :width]), jnp.sum(squares[:, width:])), ('ro...  59 us
    all_gather x1, waiting for transfers between devices, local(): projected = lax.all_gather(own_rows, 'row', axis=0, tiled=True)  54.2 us
    all_gather x1, waiting for transfers between devices, local(): both_images = lax.all_gather(own_images, 'col', axis=0, tiled=True)  21.2 us
    dot_general x2, matrix products, times_transposed(): lax.dot_general(factor_block, projected, (((1,), (1,)), ((), ())), prefer...  12.3 us
    dot_general x1, matrix products, local(): jnp.dot(grad_image, grad_proj, preferred_element_type=jnp.float32)  11.3 us
  transfers between devices with their start and end apart: 4, of which 4 were waited for; matrix products, arithmetic and copies ran while one was open for 0% of the time, Pallas kernels for 0%

commit v1 on v0

v1 whole, which is shorter than its diff:
```python
import functools

import jax
import jax.numpy as jnp
from jax import lax
from jax.experimental import pallas as pl
from jax.experimental.pallas import tpu as pltpu
from jax.sharding import PartitionSpec as P

keep_scale = 1.45
gram_scale = 0.5

CHUNKS = 2
PIECES = 4
BF16 = jnp.bfloat16
F32 = jnp.float32


def schedule(levels, units, pieces, half, tokens, rows, width):
    link, chip, latency, flops = 0.065e6, 0.25e6, 1.6, 0.8e9
    unit_bytes = tokens * width * 2
    piece_bytes = rows // pieces * tokens * 2
    free = {}
    arrive = {}

    def send(line, now, size, rate):
        begin = max(now, free.get(line, 0.0))
        free[line] = begin + size / rate
        return free[line] + latency

    stages = 2 * levels
    pending = {}
    done = {}
    for u in range(units):
        for k in range(stages + 1):
            pending["E", u, k] = [("E", u, k - 1)] if k else []
        pending["Z0", u] = [("E", u, stages)]
        pending["S", u] = [("Z0", u)]
        for r in range(pieces):
            pending["Z1", u, r] = [("Z0", u)]
            pending["Z2", u, r] = [("Z1", u, r)]
            pending["Z3", u, r] = [("Z2", u, r)]
    pending["M1",] = [("S", u) for u in range(units)]
    pending["M2",] = [("M1",)]
    first = range(units // 2)
    second = range(units // 2, units)
    pending["F0",] = [("M2",)] + [("Z3", u, r) for u in first for r in range(pieces)]
    for r in range(pieces):
        pending["F1", r] = [("M2",)] + [("Z3", u, r) for u in second]
    rank = {"E": 0, "M1": 1, "M2": 2, "Z1": 2, "Z2": 1, "Z0": 3, "S": 4, "Z3": 5, "F0": 6, "F1": 4}

    def weight(event):
        kind = event[0]
        if kind == "E" and event[2] == 0:
            return (3.5, event[1])
        return (rank[kind],) + tuple(event[1:])

    work = 2.0 * tokens * rows * width / flops
    cost = {"Z0": work, "F0": work * units / 2, "F1": work * units / 2 / pieces, "S": 1.0, "M1": 0.5, "M2": 0.5}
    now, order = 0.0, []
    while pending:
        ready = []
        for event, deps in pending.items():
            if any(d in pending for d in deps):
                continue
            at = max([arrive.get(event, 0.0)] + [done[d] for d in deps])
            ready.append((max(at, now), weight(event), event))
        at, _, event = min(ready)
        kind = event[0]
        spent = cost.get(kind, 0.3)
        if kind == "E":
            spent = work if event[2] == 0 else 0.4
        now = at + spent
        del pending[event]
        done[event] = now
        order.append(event)
        if kind == "E" and event[2] < stages:
            u, k = event[1:]
            level = k if k < levels else stages - 1 - k
            size = unit_bytes / 2 ** (level + 1)
            rate = chip if level == 0 else link
            arrive["E", u, k + 1] = send(("row", level), now, size, rate)
        elif kind == "Z0":
            for r in range(pieces):
                begin = now - spent * (1 - (r + 1) / pieces)
                arrive["Z1", event[1], r] = send("up", begin, piece_bytes, 0.047e6)
        elif kind == "Z1":
            arrive["Z2", event[1], event[2]] = send("cross", now, piece_bytes, 0.047e6)
        elif kind == "Z2":
            arrive["Z3", event[1], event[2]] = send("down", now, piece_bytes, 0.047e6)
        elif kind == "M1":
            arrive["M2",] = now + 6.0
    return order


def kernel(
    n_row, n_col, order, chunks, pieces,
    act_in, grad_in, act_k, grad_k, act_out, grad_out,
    x_v, k_v, part, proj, own, up_in, cross_in, image, squares, means, *rest,
):
    levels = n_row.bit_length() - 1
    landing = rest[:levels]
    (load_sem, store_sem, row_send, row_recv, in_send, out_send, up_recv, in_recv,
     mean_send, mean_recv) = rest[levels:]
    units, tokens, width = part.shape
    rows = k_v.shape[1]
    height = rows // pieces
    half = n_col // 2
    stages = 2 * levels
    row = lax.axis_index("row")
    col = lax.axis_index("col")

    def factor(u):
        return u // chunks

    def at(start, size, unit=16):
        return pl.ds(pl.multiple_of(start, unit), size)

    odd = lax.rem(row, 2)
    partner, mine = [], []
    for s in range(levels):
        near = 2**s
        far = 1 if s == 0 else 2 ** (levels - s)
        near_bit = lax.rem(lax.div(row, near), 2)
        far_bit = lax.rem(lax.div(row, far), 2)
        near_peer = row + near * (1 - 2 * near_bit)
        far_peer = row + far * (1 - 2 * far_bit)
        mine.append(near_bit + odd * (far_bit - near_bit))
        partner.append(near_peer + odd * (far_peer - near_peer))
    starts, sizes = [0], [tokens]
    for s in range(levels):
        sizes.append(sizes[s] // 2)
        starts.append(starts[s] + mine[s] * sizes[s + 1])
    away = [starts[s] + (1 - mine[s]) * sizes[s + 1] for s in range(levels)]

    low = 1 - lax.div(col, half)
    depth = low * col + (1 - low) * (n_col - 1 - col)
    inward = col + 2 * low - 1
    outward = col - 2 * low + 1
    inner = depth == half - 1
    not_end = depth > 0

    barrier = pltpu.get_barrier_semaphore()
    for s in range(levels):
        pl.semaphore_signal(
            barrier, inc=1, device_id={"row": partner[s]}, device_id_type=pl.DeviceIdType.MESH
        )
    for d in range(1, n_col):
        pl.semaphore_signal(
            barrier, inc=1, device_id={"col": lax.rem(col + d, n_col)},
            device_id_type=pl.DeviceIdType.MESH,
        )

    loads = []
    for f, (x, k) in enumerate(((act_in, act_k), (grad_in, grad_k))):
        loads.append((
            pltpu.make_async_copy(x, x_v.at[f], load_sem.at[f, 0]),
            pltpu.make_async_copy(k, k_v.at[f], load_sem.at[f, 1]),
        ))
    for pair in loads:
        for copy in pair:
            copy.start()

    def remote(src, dst, send_sem, recv_sem, **device):
        return pltpu.make_async_remote_copy(
            src_ref=src, dst_ref=dst, send_sem=send_sem, recv_sem=recv_sem,
            device_id=device, device_id_type=pl.DeviceIdType.MESH,
        )

    def scatter_copy(u, s):
        size = sizes[s + 1]
        return remote(
            part.at[u, at(away[s], size)], landing[s].at[u],
            row_send.at[u, s], row_recv.at[u, s], row=partner[s],
        )

    def gather_copy(u, s):
        here = proj.at[u, at(starts[s + 1], sizes[s + 1])]
        k = stages - 1 - s
        return remote(here, here, row_send.at[u, k], row_recv.at[u, k], row=partner[s])

    def gather_arrival(u, s):
        there = proj.at[u, at(away[s], sizes[s + 1])]
        k = stages - 1 - s
        return remote(there, there, row_send.at[u, k], row_recv.at[u, k], row=partner[s])

    def piece(r):
        return pl.ds(r * height if isinstance(r, int) else pl.multiple_of(r * height, height), height)

    def up_copy(u, r):
        return remote(own.at[u, piece(r)], up_in.at[u, piece(r)], in_send.at[u, r], up_recv.at[u, r], col=inward)

    def cross_copy(u, r):
        return remote(own.at[u, piece(r)], cross_in.at[u, piece(r)], in_send.at[u, r], in_recv.at[u, r], col=inward)

    def down_copy(u, r):
        return remote(image.at[u, piece(r)], image.at[u, piece(r)], out_send.at[u, r], in_recv.at[u, r], col=outward)

    def send_inward(u, r):
        @pl.when(inner)
        def _():
            cross_copy(u, r).start()

        if half > 1:
            @pl.when(jnp.logical_not(inner))
            def _():
                up_copy(u, r).start()

    def mean_copy(d):
        to = lax.rem(col + d, n_col)
        return remote(means.at[col], means.at[col], mean_send.at[d], mean_recv.at[d], col=to)

    def mean_arrival(d):
        source = lax.rem(col + n_col - d, n_col)
        return remote(means.at[source], means.at[source], mean_send.at[d], mean_recv.at[d], col=source)

    step = min(512, width)
    scale = [None, None]
    entered = [False]
    loaded = [False, False]
    outs = (act_out, grad_out)
    stores = []

    def add_part(u, s, start, size):
        offset = start - starts[s + 1]
        tile = min(size, 64)

        @pl.loop(0, size // tile)
        def _(i):
            a = at(start + i * tile, tile)
            b = at(offset + i * tile, tile)
            part[u, a, :] = (part[u, a, :].astype(F32) + landing[s][u, b, :].astype(F32)).astype(BF16)

    def run_e(u, k):
        f = factor(u)
        if k == 0:
            if not loaded[f]:
                loaded[f] = True
                for copy in loads[f]:
                    copy.wait()
            base = (u % chunks) * tokens
            size = sizes[1]
            other = away[0]
            keep = starts[1]
            for start in (other, keep):
                @pl.loop(0, width // step)
                def _(j, start=start):
                    c = at(j * step, step, step)
                    part[u, at(start, size), c] = jnp.dot(
                        x_v[f, at(base + start, size), :], k_v[f, :, c], preferred_element_type=F32
                    ).astype(BF16)
                if start is other:
                    if not entered[0]:
                        entered[0] = True
                        pl.semaphore_wait(barrier, levels + n_col - 1)
                    scatter_copy(u, 0).start()
        elif k < levels:
            scatter_copy(u, k - 1).wait_recv()
            add_part(u, k - 1, away[k], sizes[k + 1])
            scatter_copy(u, k).start()
            add_part(u, k - 1, starts[k + 1], sizes[k + 1])
        elif k == levels:
            scatter_copy(u, k - 1).wait_recv()
            a = at(starts[levels], sizes[levels])
            proj[u, a, :] = (
                part[u, a, :].astype(F32) + landing[levels - 1][u].astype(F32)
            ).astype(BF16)
            gather_copy(u, levels - 1).start()
        elif k < stages:
            s = stages - k
            gather_arrival(u, s).wait_recv()
            gather_copy(u, s - 1).start()
        else:
            gather_arrival(u, 0).wait_recv()

    def run_squares(u):
        f = factor(u)
        tile = min(64, tokens)

        @pl.loop(0, tokens // tile)
        def _(i):
            p = proj[u, at(i * tile, tile), :].astype(F32)
            squares[f] += jnp.sum(jnp.square(p).reshape(tile // 8, 8, width), axis=0)

    def run_z0(u):
        f = factor(u)
        block = min(256, tokens)

        @pl.loop(0, pieces)
        def _(r):
            @pl.loop(0, tokens // block)
            def _(j):
                c = at(j * block, block, block)
                own[u, piece(r), c] = lax.dot_general(
                    k_v[f, piece(r), :], proj[u, c, :], (((1,), (1,)), ((), ())),
                    preferred_element_type=F32,
                ).astype(BF16)

            @pl.when(depth == 0)
            def _():
                send_inward(u, r)

    def run_z1(u, r):
        @pl.when(not_end)
        def _():
            up_copy(u, r).wait_recv()
            a = piece(r)
            own[u, a, :] = (own[u, a, :].astype(F32) + up_in[u, a, :].astype(F32)).astype(BF16)
            send_inward(u, r)

    def run_z2(u, r):
        @pl.when(inner)
        def _():
            cross_copy(u, r).wait_recv()
            a = piece(r)
            image[u, a, :] = (own[u, a, :].astype(F32) + cross_in[u, a, :].astype(F32)).astype(BF16)

            @pl.when(not_end)
            def _():
                down_copy(u, r).start()

    def run_z3(u, r):
        @pl.when(jnp.logical_not(inner))
        def _():
            down_copy(u, r).wait_recv()

            @pl.when(not_end)
            def _():
                down_copy(u, r).start()

    def run_m1():
        for f in range(2):
            total = squares[f, :, :128]
            for j in range(1, width // 128):
                total = total + squares[f, :, j * 128 : (j + 1) * 128]
            means[col, f] = total
        for d in range(1, n_col):
            mean_copy(d).start()

    def run_m2():
        for d in range(1, n_col):
            mean_arrival(d).wait_recv()
        entries = chunks * tokens * width * n_col
        for f in range(2):
            total = means[0, f]
            for j in range(1, n_col):
                total = total + means[j, f]
            scale[1 - f] = gram_scale / (chunks * tokens) * (jnp.sum(total) / entries)

    def change(f, r):
        @pl.loop(0, width // step)
        def _(j):
            c = at(j * step, step, step)
            total = None
            for u in range(f * chunks, (f + 1) * chunks):
                term = jnp.dot(image[u, piece(r), :], proj[u, :, c], preferred_element_type=F32)
                total = term if total is None else total + term
            k_v[f, piece(r), c] = (
                keep_scale * k_v[f, piece(r), c].astype(F32) - scale[f] * total
            ).astype(BF16)

    def run_f(f, r):
        if f == 0:
            @pl.loop(0, pieces)
            def _(i):
                change(0, i)

            copy = pltpu.make_async_copy(k_v.at[0], outs[0], store_sem.at[pieces])
        else:
            change(1, r)
            copy = pltpu.make_async_copy(k_v.at[1, piece(r)], outs[1].at[piece(r)], store_sem.at[r])
        copy.start()
        stores.append(copy)

    squares[...] = jnp.zeros(squares.shape, F32)
    for event in order:
        kind = event[0]
        if kind == "S":
            run_squares(event[1])
        elif kind == "E":
            run_e(event[1], event[2])
        elif kind == "Z0":
            run_z0(event[1])
        elif kind == "Z1":
            run_z1(*event[1:])
        elif kind == "Z2":
            run_z2(*event[1:])
        elif kind == "Z3":
            run_z3(*event[1:])
        elif kind == "M1":
            run_m1()
        elif kind == "M2":
            run_m2()
        elif kind == "F0":
            run_f(0, None)
        else:
            run_f(1, event[1])

    for u in range(units):
        for s in range(levels):
            scatter_copy(u, s).wait_send()
            gather_copy(u, s).wait_send()

        @pl.loop(0, pieces)
        def _(r, u=u):
            cross_copy(u, r).wait_send()

            @pl.when(not_end)
            def _():
                down_copy(u, r).wait_send()
    for d in range(1, n_col):
        mean_copy(d).wait_send()
    for copy in stores:
        copy.wait()


def local(n_row, n_col, activations, cotangents, act_factor, grad_factor):
    rows, width = act_factor.shape
    tokens = activations.shape[0] // CHUNKS
    units = 2 * CHUNKS
    levels = n_row.bit_length() - 1
    order = schedule(levels, units, PIECES, n_col // 2, tokens, rows, width)
    dma = pltpu.SemaphoreType.DMA
    anywhere = pl.BlockSpec(memory_space=pl.ANY)
    return pl.pallas_call(
        functools.partial(kernel, n_row, n_col, order, CHUNKS, PIECES),
        out_shape=[jax.ShapeDtypeStruct((rows, width), BF16)] * 2,
        in_specs=[anywhere] * 4,
        out_specs=[anywhere] * 2,
        scratch_shapes=[
            pltpu.VMEM((2,) + activations.shape, BF16),
            pltpu.VMEM((2, rows, width), BF16),
            pltpu.VMEM((units, tokens, width), BF16),
            pltpu.VMEM((units, tokens, width), BF16),
            pltpu.VMEM((units, rows, tokens), BF16),
            pltpu.VMEM((units, rows, tokens), BF16),
            pltpu.VMEM((units, rows, tokens), BF16),
            pltpu.VMEM((units, rows, tokens), BF16),
            pltpu.VMEM((2, 8, width), F32),
            pltpu.VMEM((n_col, 2, 8, 128), F32),
        ]
        + [pltpu.VMEM((units, tokens >> (s + 1), width), BF16) for s in range(levels)]
        + [
            dma((2, 2)),
            dma((PIECES + 1,)),
            dma((units, 2 * levels)),
            dma((units, 2 * levels)),
            dma((units, PIECES)),
            dma((units, PIECES)),
            dma((units, PIECES)),
            dma((units, PIECES)),
            dma((n_col,)),
            dma((n_col,)),
        ],
        compiler_params=pltpu.CompilerParams(
            collective_id=0, has_side_effects=True, vmem_limit_bytes=67043328
        ),
    )(activations, cotangents, act_factor, grad_factor)


def solution(mesh):
    return jax.shard_map(
        functools.partial(local, mesh.shape["row"], mesh.shape["col"]),
        mesh=mesh,
        in_specs=(P(None, "row"), P(None, "row"), P("row", "col"), P("row", "col")),
        out_specs=(P("row", "col"), P("row", "col")),
        check_vma=False,
    )
```

time: 476 us -> 257 us (0.54)
  waiting for transfers between devices: 339 us -> 0 us
  Pallas kernels: 0 us -> 249 us
  blocking collectives: 59 us -> 0 us
  matrix products: 43.6 us -> 0 us
  other arithmetic: 16.7 us -> 0 us
  between operations: 15.1 us -> 0.65 us
  local copies, waits for them, and re-layouts: 1.57 us -> 6.96 us
    reduce_scatter x2 -> x0, waiting for transfers between devices: 264 us -> none  [the longest x1 145 us: local(): lax.psum_scatter(jnp.concatenate([times_transposed(act_factor, act_proj),...]
    pallas_call x0 -> x1, Pallas kernels: none -> 249 us  [local(): pl.pallas_call(functools.partial(kernel, n_row, n_col, order, CHUNKS, PIE...]
    all_gather x2 -> x0, waiting for transfers between devices: 75.4 us -> none  [the longest x1 54.2 us: local(): projected = lax.all_gather(own_rows, 'row', axis=0, tiled=True)]
    psum x1 -> x0, blocking collectives: 59 us -> none  [local(): lax.psum((jnp.sum(squares[:, :width]), jnp.sum(squares[:, width:])), ('ro...]
    dot_general x6 -> x0, matrix products: 43.6 us -> none  [the longest x2 12.3 us: times_transposed(): lax.dot_general(factor_block, projected, (((1,), (1,)), ((), ())), prefer...]
    concatenate x2 -> x0, other arithmetic: 10.3 us -> none  [the longest x1 6.23 us: local(): jnp.concatenate([jnp.dot(activations, act_factor, preferred_element_type=...]
    unnamed x16 -> x4, local copies, waits for them, and re-layouts: 1.57 us -> 6.96 us
  transfers between devices with their start and end apart: 4 -> 0, of which waited for: 4 -> 0; matrix products, arithmetic and copies ran while one was open for 0% -> 0% of each run, Pallas kernels for 0% -> 0%
where the time goes in v1:
time: 257 us
  Pallas kernels  249 us (97%)
  local copies, waits for them, and re-layouts  6.96 us (3%)
    pallas_call x1, Pallas kernels, local(): pl.pallas_call(functools.partial(kernel, n_row, n_col, order, CHUNKS, PIE...  249 us
    unnamed x4, local copies, waits for them, and re-layouts  6.96 us

profile of v1, /device:TPU:0, one launch (start us, length us, event | category | flops | bytes accessed | tf_op | source)
XLA Modules:
  0.0 257.1 jit_solution(4658125606716683270)
XLA Ops:
  0.6 249.5 %shard_map.59 = (bf16[1024,2048]{1,0:T(8,128)(2,1)}, bf16[1024,2048]{1,0:T(8,128)(2,1)}) custom-call(bf16[1024,1024]{1,0:T(8,128)(2,1)} %act_in.1, bf16[1024,1024]{1,0:T(8,128)(2,1)} %grad_in.1, bf16[1024,2048]{1,0:T(8,128)(2,1)} %act_k.1, bf16[1024,2048]{1,0:T(8,128)(2,1)} %grad_k.1), custom_call_target="tpu_custom_call" | custom-call | tf_op jit(solution)/shard_map/pallas_call | solution.py:425
  250.1 0.0 copy-start
  250.1 4.9 %copy.8 = bf16[1024,2048]{1,0:T(8,128)(2,1)} copy(bf16[1024,2048]{1,0:T(8,128)(2,1)} %get-tuple-element.4) | data formatting | bytes 8388608
  255.1 0.0 copy-done
  255.1 2.0 copy.9
Async XLA Ops:
  250.1 5.0 %copy-start = (bf16[1024,2048]{1,0:T(8,128)(2,1)S(1)}, bf16[1024,2048]{1,0:T(8,128)(2,1)}, u32[]{:S(2)}) copy-start(bf16[1024,2048]{1,0:T(8,128)(2,1)} %get-tuple-element.5) | copy-start | bytes 12582916

commit v2 on v1

--- a/solution.py
+++ b/solution.py
@@ -12,6 +12,7 @@
 
 CHUNKS = 2
 PIECES = 4
+WINDOW = 2
 BF16 = jnp.bfloat16
 F32 = jnp.float32
 
@@ -96,13 +97,14 @@
 def kernel(
     n_row, n_col, order, chunks, pieces,
     act_in, grad_in, act_k, grad_k, act_out, grad_out,
-    x_v, k_v, part, proj, own, up_in, cross_in, image, squares, means, *rest,
+    x_v, k_v, kept, proj, own, up, image, squares, means, *rest,
 ):
     levels = n_row.bit_length() - 1
     landing = rest[:levels]
+    leaving = rest[levels : 2 * levels]
     (load_sem, store_sem, row_send, row_recv, in_send, out_send, up_recv, in_recv,
-     mean_send, mean_recv) = rest[levels:]
-    units, tokens, width = part.shape
+     mean_send, mean_recv) = rest[2 * levels :]
+    units, tokens, width = proj.shape
     rows = k_v.shape[1]
     height = rows // pieces
     half = n_col // 2
@@ -168,9 +170,8 @@
         )
 
     def scatter_copy(u, s):
-        size = sizes[s + 1]
         return remote(
-            part.at[u, at(away[s], size)], landing[s].at[u],
+            leaving[s].at[u], landing[s].at[u],
             row_send.at[u, s], row_recv.at[u, s], row=partner[s],
         )
 
@@ -188,10 +189,10 @@
         return pl.ds(r * height if isinstance(r, int) else pl.multiple_of(r * height, height), height)
 
     def up_copy(u, r):
-        return remote(own.at[u, piece(r)], up_in.at[u, piece(r)], in_send.at[u, r], up_recv.at[u, r], col=inward)
+        return remote(up.at[u, piece(r)], up.at[u, piece(r)], in_send.at[u, r], up_recv.at[u, r], col=inward)
 
     def cross_copy(u, r):
-        return remote(own.at[u, piece(r)], cross_in.at[u, piece(r)], in_send.at[u, r], in_recv.at[u, r], col=inward)
+        return remote(up.at[u, piece(r)], image.at[u, piece(r)], in_send.at[u, r], in_recv.at[u, r], col=inward)
 
     def down_copy(u, r):
         return remote(image.at[u, piece(r)], image.at[u, piece(r)], out_send.at[u, r], in_recv.at[u, r], col=outward)
@@ -220,16 +221,21 @@
     loaded = [False, False]
     outs = (act_out, grad_out)
     stores = []
-
-    def add_part(u, s, start, size):
+    paced = []
+
+    def add_kept(u, s, start, size, into):
+        inside = start - starts[1]
         offset = start - starts[s + 1]
         tile = min(size, 64)
 
         @pl.loop(0, size // tile)
         def _(i):
-            a = at(start + i * tile, tile)
-            b = at(offset + i * tile, tile)
-            part[u, a, :] = (part[u, a, :].astype(F32) + landing[s][u, b, :].astype(F32)).astype(BF16)
+            a = at(inside + i * tile, tile)
+            total = kept[u, a, :] + landing[s][u, at(offset + i * tile, tile), :].astype(F32)
+            if into is None:
+                kept[u, a, :] = total
+            else:
+                into[u, pl.ds(pl.multiple_of(i * tile, tile), tile), :] = total.astype(BF16)
 
     def run_e(u, k):
         f = factor(u)
@@ -246,9 +252,13 @@
                 @pl.loop(0, width // step)
                 def _(j, start=start):
                     c = at(j * step, step, step)
-                    part[u, at(start, size), c] = jnp.dot(
+                    product = jnp.dot(
                         x_v[f, at(base + start, size), :], k_v[f, :, c], preferred_element_type=F32
-                    ).astype(BF16)
+                    )
+                    if start is other:
+                        leaving[0][u, :, c] = product.astype(BF16)
+                    else:
+                        kept[u, :, c] = product
                 if start is other:
                     if not entered[0]:
                         entered[0] = True
@@ -256,15 +266,14 @@
                     scatter_copy(u, 0).start()
         elif k < levels:
             scatter_copy(u, k - 1).wait_recv()
-            add_part(u, k - 1, away[k], sizes[k + 1])
+            add_kept(u, k - 1, away[k], sizes[k + 1], leaving[k])
             scatter_copy(u, k).start()
-            add_part(u, k - 1, starts[k + 1], sizes[k + 1])
+            add_kept(u, k - 1, starts[k + 1], sizes[k + 1], None)
         elif k == levels:
             scatter_copy(u, k - 1).wait_recv()
             a = at(starts[levels], sizes[levels])
-            proj[u, a, :] = (
-                part[u, a, :].astype(F32) + landing[levels - 1][u].astype(F32)
-            ).astype(BF16)
+            inside = at(starts[levels] - starts[1], sizes[levels])
+            proj[u, a, :] = (kept[u, inside, :] + landing[levels - 1][u].astype(F32)).astype(BF16)
             gather_copy(u, levels - 1).start()
         elif k < stages:
             s = stages - k
@@ -291,21 +300,38 @@
             @pl.loop(0, tokens // block)
             def _(j):
                 c = at(j * block, block, block)
-                own[u, piece(r), c] = lax.dot_general(
+                product = lax.dot_general(
                     k_v[f, piece(r), :], proj[u, c, :], (((1,), (1,)), ((), ())),
                     preferred_element_type=F32,
-                ).astype(BF16)
-
-            @pl.when(depth == 0)
-            def _():
-                send_inward(u, r)
+                )
+
+                @pl.when(not_end)
+                def _():
+                    own[u, piece(r), c] = product
+
+                @pl.when(depth == 0)
+                def _():
+                    up[u, piece(r), c] = product.astype(BF16)
+
+                    if half == 1:
+                        own[u, piece(r), c] = product
 
     def run_z1(u, r):
+        @pl.when(depth == 0)
+        def _():
+            if len(paced) >= WINDOW:
+                cross_copy(*paced[-WINDOW]).wait_send()
+            send_inward(u, r)
+
+        paced.append((u, r))
+
         @pl.when(not_end)
         def _():
             up_copy(u, r).wait_recv()
             a = piece(r)
-            own[u, a, :] = (own[u, a, :].astype(F32) + up_in[u, a, :].astype(F32)).astype(BF16)
+            total = own[u, a, :] + up[u, a, :].astype(F32)
+            own[u, a, :] = total
+            up[u, a, :] = total.astype(BF16)
             send_inward(u, r)
 
     def run_z2(u, r):
@@ -313,19 +339,17 @@
         def _():
             cross_copy(u, r).wait_recv()
             a = piece(r)
-            image[u, a, :] = (own[u, a, :].astype(F32) + cross_in[u, a, :].astype(F32)).astype(BF16)
+            image[u, a, :] = (own[u, a, :] + image[u, a, :].astype(F32)).astype(BF16)
 
             @pl.when(not_end)
             def _():
                 down_copy(u, r).start()
 
     def run_z3(u, r):
-        @pl.when(jnp.logical_not(inner))
-        def _():
-            down_copy(u, r).wait_recv()
-
-            @pl.when(not_end)
+        if half > 2:
+            @pl.when(jnp.logical_and(not_end, jnp.logical_not(inner)))
             def _():
+                down_copy(u, r).wait_recv()
                 down_copy(u, r).start()
 
     def run_m1():
@@ -348,6 +372,12 @@
             scale[1 - f] = gram_scale / (chunks * tokens) * (jnp.sum(total) / entries)
 
     def change(f, r):
+        if half > 1:
+            @pl.when(depth == 0)
+            def _():
+                for u in range(f * chunks, (f + 1) * chunks):
+                    down_copy(u, r).wait_recv()
+
         @pl.loop(0, width // step)
         def _(j):
             c = at(j * step, step, step)
@@ -401,13 +431,17 @@
             scatter_copy(u, s).wait_send()
             gather_copy(u, s).wait_send()
 
-        @pl.loop(0, pieces)
-        def _(r, u=u):
+    for i, (u, r) in enumerate(paced):
+        if i + WINDOW >= len(paced):
             cross_copy(u, r).wait_send()
-
+        else:
             @pl.when(not_end)
-            def _():
-                down_copy(u, r).wait_send()
+            def _(u=u, r=r):
+                cross_copy(u, r).wait_send()
+
+        @pl.when(not_end)
+        def _(u=u, r=r):
+            down_copy(u, r).wait_send()
     for d in range(1, n_col):
         mean_copy(d).wait_send()
     for copy in stores:
@@ -430,16 +464,15 @@
         scratch_shapes=[
             pltpu.VMEM((2,) + activations.shape, BF16),
             pltpu.VMEM((2, rows, width), BF16),
+            pltpu.VMEM((units, tokens // 2, width), F32),
             pltpu.VMEM((units, tokens, width), BF16),
-            pltpu.VMEM((units, tokens, width), BF16),
-            pltpu.VMEM((units, rows, tokens), BF16),
-            pltpu.VMEM((units, rows, tokens), BF16),
+            pltpu.VMEM((units, rows, tokens), F32),
             pltpu.VMEM((units, rows, tokens), BF16),
             pltpu.VMEM((units, rows, tokens), BF16),
             pltpu.VMEM((2, 8, width), F32),
             pltpu.VMEM((n_col, 2, 8, 128), F32),
         ]
-        + [pltpu.VMEM((units, tokens >> (s + 1), width), BF16) for s in range(levels)]
+        + [pltpu.VMEM((units, tokens >> (s + 1), width), BF16) for s in range(levels)] * 2
         + [
             dma((2, 2)),
             dma((PIECES + 1,)),

time: 257 us -> 212 us (0.82)
  Pallas kernels: 249 us -> 203 us
    pallas_call x1, Pallas kernels: 249 us -> 203 us  [local(): pl.pallas_call(functools.partial(kernel, n_row, n_col, order, CHUNKS, PIE...]
where the time goes in v2:
time: 212 us; the launch traced here: 210 us
  Pallas kernels  203 us (96%)
  local copies, waits for them, and re-layouts  6.96 us (3%)
    pallas_call x1, Pallas kernels, local(): pl.pallas_call(functools.partial(kernel, n_row, n_col, order, CHUNKS, PIE...  203 us
    unnamed x4, local copies, waits for them, and re-layouts  6.96 us

profile of v2, /device:TPU:0, one launch (start us, length us, event | category | flops | bytes accessed | tf_op | source)
XLA Modules:
  0.0 210.2 jit_solution(1636468995224593005)
XLA Ops:
  0.6 202.6 %shard_map.59 = (bf16[1024,2048]{1,0:T(8,128)(2,1)}, bf16[1024,2048]{1,0:T(8,128)(2,1)}) custom-call(bf16[1024,1024]{1,0:T(8,128)(2,1)} %act_in.1, bf16[1024,1024]{1,0:T(8,128)(2,1)} %grad_in.1, bf16[1024,2048]{1,0:T(8,128)(2,1)} %act_k.1, bf16[1024,2048]{1,0:T(8,128)(2,1)} %grad_k.1), custom_call_target="tpu_custom_call" | custom-call | tf_op jit(solution)/shard_map/pallas_call | solution.py:459
  203.3 0.0 copy-start
  203.3 4.9 %copy.8 = bf16[1024,2048]{1,0:T(8,128)(2,1)} copy(bf16[1024,2048]{1,0:T(8,128)(2,1)} %get-tuple-element.4) | data formatting | bytes 8388608
  208.2 0.0 copy-done
  208.2 2.0 copy.9
Async XLA Ops:
  203.3 5.0 %copy-start = (bf16[1024,2048]{1,0:T(8,128)(2,1)S(1)}, bf16[1024,2048]{1,0:T(8,128)(2,1)}, u32[]{:S(2)}) copy-start(bf16[1024,2048]{1,0:T(8,128)(2,1)} %get-tuple-element.5) | copy-start | bytes 12582916

commit v3 on v2

--- a/solution.py
+++ b/solution.py
@@ -10,7 +10,7 @@
 keep_scale = 1.45
 gram_scale = 0.5
 
-CHUNKS = 2
+CHUNKS = 4
 PIECES = 4
 WINDOW = 2
 BF16 = jnp.bfloat16
@@ -35,6 +35,10 @@
     for u in range(units):
         for k in range(stages + 1):
             pending["E", u, k] = [("E", u, k - 1)] if k else []
+            if k == 1 and u >= 1:
+                pending["E", u, k].append(("E", u - 1, 2))
+            if k == 1 and u >= 2:
+                pending["E", u, k].append(("E", u - 2, stages))
         pending["Z0", u] = [("E", u, stages)]
         pending["S", u] = [("Z0", u)]
         for r in range(pieces):

time: 212 us -> 183 us (0.86)
  Pallas kernels: 203 us -> 176 us
    pallas_call x1, Pallas kernels: 203 us -> 176 us  [local(): pl.pallas_call(functools.partial(kernel, n_row, n_col, order, CHUNKS, PIE...]
where the time goes in v3:
time: 183 us
  Pallas kernels  176 us (96%)
  local copies, waits for them, and re-layouts  6.96 us (4%)
    pallas_call x1, Pallas kernels, local(): pl.pallas_call(functools.partial(kernel, n_row, n_col, order, CHUNKS, PIE...  176 us
    unnamed x4, local copies, waits for them, and re-layouts  6.96 us

profile of v3, /device:TPU:0, one launch (start us, length us, event | category | flops | bytes accessed | tf_op | source)
XLA Modules:
  0.0 183.1 jit_solution(14084674226191208328)
XLA Ops:
  0.6 175.5 %shard_map.59 = (bf16[1024,2048]{1,0:T(8,128)(2,1)}, bf16[1024,2048]{1,0:T(8,128)(2,1)}) custom-call(bf16[1024,1024]{1,0:T(8,128)(2,1)} %act_in.1, bf16[1024,1024]{1,0:T(8,128)(2,1)} %grad_in.1, bf16[1024,2048]{1,0:T(8,128)(2,1)} %act_k.1, bf16[1024,2048]{1,0:T(8,128)(2,1)} %grad_k.1), custom_call_target="tpu_custom_call" | custom-call | tf_op jit(solution)/shard_map/pallas_call | solution.py:463
  176.2 0.0 copy-start
  176.2 4.9 %copy.8 = bf16[1024,2048]{1,0:T(8,128)(2,1)} copy(bf16[1024,2048]{1,0:T(8,128)(2,1)} %get-tuple-element.4) | data formatting | bytes 8388608
  181.1 0.0 copy-done
  181.1 2.0 %copy.9 = bf16[1024,2048]{1,0:T(8,128)(2,1)} copy(bf16[1024,2048]{1,0:T(8,128)(2,1)S(1)} %copy-done) | data formatting | bytes 8388608
Async XLA Ops:
  176.2 5.0 %copy-start = (bf16[1024,2048]{1,0:T(8,128)(2,1)S(1)}, bf16[1024,2048]{1,0:T(8,128)(2,1)}, u32[]{:S(2)}) copy-start(bf16[1024,2048]{1,0:T(8,128)(2,1)} %get-tuple-element.5) | copy-start | bytes 12582916
